TPU v7x, 32 devices: a whole 2x2x4 slice. The times are simulated.
32 devices in a mesh: blk: 8 (over z, y), lblk: 4 (over x, core).
Axes of the slice: x: 2, y: 2, z: 4, core: 2. Of those that a mesh axis runs over, the one named last changes fastest.
Arguments:
- sky: bfloat16 [8, 2, 32, 16384], P(None, None, 'blk', 'lblk'), may hold values from -6 to 6
- arc_start: int32 [2, 32], P(None, 'blk'), may hold values from 0 to 16383
- arc_count: int32 [2, 32], P(None, 'blk'), may hold values from 4096 to 16384
- owner_modes: int32 [32], replicated, may hold values from 0 to 31, each once
- legendre: bfloat16 [32, 8, 4, 4096], P('blk', None, None, 'lblk'), may hold values from -1 to 1
Outputs:
- alm: float32 [8, 2, 32, 4096], P(None, None, 'blk', 'lblk')
Inputs may be any that keep to these rules, and one draw needn't show every extreme that they name: `owner_modes`: each m-mode 0 to 31 appears exactly once.
All inputs are finite; a program needn't handle non-finite values.
Results may differ from a plain program's by a relative error of at most 0.0049.
Values may be sent and summed in bfloat16 or wider, within the bound.
No kernel may reach another device: no remote copies, remote signals or barrier semaphores. Data moves between devices by JAX's collectives and lax.ppermute only.
A program may use at most 64 MiB of HBM per device.

v0:
```python
import math
import jax
import jax.numpy as jnp
from jax import lax
from jax.sharding import PartitionSpec as P

RLEN = 16384
DIFFUSION = 0.2


def padded(x, sides, width, wrap):
    for axis, dim in sides:
        count, length = (lax.axis_size(axis), x.shape[dim])
        up = [(i, (i + 1) % count) for i in range(count if wrap else count - 1)]
        down = [(j, i) for i, j in up]
        last = lax.slice_in_dim(x, length - width, length, axis=dim)
        initial = lax.slice_in_dim(x, 0, width, axis=dim)
        before = lax.ppermute(last, axis, up)
        after = lax.ppermute(initial, axis, down)
        x = jnp.concatenate([before, x, after], axis=dim)
    return x


def mode_basis(positions, mode_list):
    product_index = jnp.mod(positions[:, None] * mode_list[None, :], RLEN)
    angles = 2.0 * math.pi / RLEN * product_index.astype(jnp.float32)
    return (jnp.cos(angles).astype(jnp.bfloat16), (-jnp.sin(angles)).astype(jnp.bfloat16))


def legendre_section(fourier, legendre_rows, my_modes, degrees):
    north_part = fourier[:, 0].astype(jnp.float32)
    south_part = fourier[:, 1].astype(jnp.float32)
    folded = jnp.concatenate([north_part + south_part, north_part - south_part], axis=2).astype(
        jnp.bfloat16
    )
    latitude_sums = jnp.einsum(
        "xrys,srl->xysl", folded, legendre_rows, preferred_element_type=jnp.float32
    )
    even_parity = jnp.mod(degrees[None, :] + my_modes[:, None], 2) == 0
    chosen = jnp.where(even_parity[None, None], latitude_sums[:, :2], latitude_sums[:, 2:])
    inside = (degrees[None, :] >= my_modes[:, None])[None, None]
    return jnp.where(inside, chosen, jnp.zeros((), jnp.float32))


def local(sky, arc_start, arc_count, owner_modes, legendre):
    maps_here = sky.shape[0]
    band_here = sky.shape[2]
    quarter = sky.shape[3]
    column = lax.axis_index("lblk")
    positions = column * quarter + jnp.arange(quarter, dtype=jnp.int32)
    offset = jnp.mod(positions[None, None, :] - arc_start[:, :, None], RLEN)
    kept_mask = offset < arc_count[:, :, None]
    masked = jnp.where(kept_mask[None], sky, jnp.zeros((), jnp.bfloat16))
    layered = padded(masked, (("blk", 2),), 1, False)
    edge_padded = padded(masked, (("lblk", 3),), 1, True)
    is_last = lax.axis_index("blk") == lax.axis_size("blk") - 1
    beyond = jnp.where(is_last, masked[:, ::-1, band_here - 1 :], layered[:, :, band_here + 1 :])
    centre = masked.astype(jnp.float32)
    layer_above = layered[:, :, :band_here].astype(jnp.float32)
    layer_below = jnp.concatenate([layered[:, :, 2 : band_here + 1], beyond], axis=2).astype(
        jnp.float32
    )
    pixel_before = edge_padded[:, :, :, :quarter].astype(jnp.float32)
    pixel_after = edge_padded[:, :, :, 2:].astype(jnp.float32)
    total = layer_above + layer_below + pixel_before + pixel_after - 4.0 * centre
    smooth = (centre + DIFFUSION * total).astype(jnp.bfloat16)
    cos_table, sin_table = mode_basis(positions, owner_modes)
    slab_size = owner_modes.shape[0]
    flat_rows = smooth.reshape(maps_here * 2 * band_here, quarter)
    real_part = jnp.dot(flat_rows, cos_table, preferred_element_type=jnp.float32).reshape(
        maps_here, 2, band_here, slab_size
    )
    imag_part = jnp.dot(flat_rows, sin_table, preferred_element_type=jnp.float32).reshape(
        maps_here, 2, band_here, slab_size
    )
    parity = jnp.arange(band_here, dtype=jnp.int32) % 2
    phase_turn = math.pi / RLEN * (parity[:, None] * owner_modes[None, :]).astype(jnp.float32)
    turn_cos = jnp.cos(phase_turn)
    turn_sin = jnp.sin(phase_turn)
    norm_scale = 1.0 / math.sqrt(RLEN)
    rotated_real = (real_part * turn_cos + imag_part * turn_sin) * norm_scale
    rotated_imag = (imag_part * turn_cos - real_part * turn_sin) * norm_scale
    partial_value = jnp.stack([rotated_real, rotated_imag], axis=3)
    owned_count = legendre.shape[0]
    degree_part = legendre.shape[3]
    my_modes = lax.dynamic_slice_in_dim(
        owner_modes, lax.axis_index("blk") * owned_count, owned_count
    )
    degrees = column * degree_part + jnp.arange(degree_part, dtype=jnp.int32)
    legendre_rows = legendre.reshape(owned_count, -1, degree_part)
    spread = lax.all_to_all(partial_value, "blk", split_axis=4, concat_axis=2, tiled=True)
    summed = lax.psum(spread, "lblk")
    fourier = summed.astype(jnp.bfloat16)
    result = legendre_section(fourier, legendre_rows, my_modes, degrees)
    return result


def solution(mesh):
    return jax.shard_map(
        local,
        mesh=mesh,
        in_specs=(
            P(None, None, "blk", "lblk"),
            P(None, "blk"),
            P(None, "blk"),
            P(),
            P("blk", None, None, "lblk"),
        ),
        out_specs=P(None, None, "blk", "lblk"),
        check_vma=False,
    )
```

profile of v0, /device:TPU:0, one launch (start us, length us, event | category | flops | bytes accessed | tf_op | source)
XLA Modules:
  0.0 53.8 jit_solution(13409327666316147105)
XLA Ops:
  0.0 0.7 %copy-done.1 = s32[2,4]{1,0:T(2,128)S(1)} copy-done((s32[2,4]{1,0:T(2,128)S(1)}, s32[2,4]{1,0:T(2,128)}, u32[]{:S(2)}) %copy-start.1) | copy-done | bytes 56
  0.7 0.2 fusion.16
  0.9 1.3 %broadcast_select_fusion.1 = bf16[8,2,4,4096]{3,2,1,0:T(4,128)(2,1)S(1)} fusion(bf16[8,2,4,4096]{3,2,1,0:T(4,128)(2,1)} %param.5, pred[2,4,4096]{2,1,0:T(4,128)(4,1)S(1)} %fusion.16), kind=kLoop, calls=%fused_computation.20 | loop fusion | flops 262144 | bytes 1081344 | tf_op jit(solution)/shard_map/jit(_where)/select_n | solution.py:53
  2.2 0.6 %fusion.38 = (bf16[8,2,1,4096]{3,2,1,0:T(2,128)(2,1)S(1)}, bf16[8,2,1,4096]{3,2,1,0:T(2,128)(2,1)S(1)}) fusion(bf16[8,2,4,4096]{3,2,1,0:T(4,128)(2,1)S(1)} %broadcast_select_fusion.1), kind=kLoop, calls=%fused_computation.70 | loop fusion | bytes 524288 | tf_op jit(solution)/shard_map/slice | solution.py:17
  2.8 1.3 %collective-permute-start.1 = (bf16[8,2,1,4096]{3,2,1,0:T(2,128)(2,1)S(1)}, bf16[8,2,1,4096]{3,2,1,0:T(2,128)(2,1)S(1)}, u32[]{:S(2)}, u32[]{:S(2)}) collective-permute-start(bf16[8,2,1,4096]{3,2,1,0:T(2,128)(2,1)S(1)} %get-tuple-element.5), channel_id=1, source_target_pairs={{4,0},{8,4},{12,8},{16,12},{20,16},{24,20},{28,24},{5,1},{9,5},{13... | collective-permute-start | bytes 393224 | tf_op jit(solution)/shard_map/ppermute | solution.py:19
  4.1 5.5 %collective-permute-start = (bf16[8,2,1,4096]{3,2,1,0:T(2,128)(2,1)S(1)}, bf16[8,2,1,4096]{3,2,1,0:T(2,128)(2,1)S(1)}, u32[]{:S(2)}, u32[]{:S(2)}) collective-permute-start(bf16[8,2,1,4096]{3,2,1,0:T(2,128)(2,1)S(1)} %get-tuple-element.6), channel_id=1, source_target_pairs={{0,4},{4,8},{8,12},{12,16},{16,20},{20,24},{24,28},{1,5},{5,9},{9,... | collective-permute-start | bytes 393224 | tf_op jit(solution)/shard_map/ppermute | solution.py:18
  9.8 1.7 %collective-permute-start.3 = (bf16[8,2,4,1]{3,2,1,0:T(4,128)(2,1)S(1)}, bf16[8,2,4,1]{3,2,1,0:T(4,128)(2,1)S(1)}, u32[]{:S(2)}, u32[]{:S(2)}) collective-permute-start(bf16[8,2,4,1]{3,2,1,0:T(4,128)(2,1)S(1)} %get-tuple-element.8), channel_id=1, source_target_pairs={{1,0},{2,1},{3,2},{0,3},{5,4},{6,5},{7,6},{4,7},{9,8},{10,9},{11,1... | collective-permute-start | bytes 392 | tf_op jit(solution)/shard_map/ppermute | solution.py:19
  11.6 0.3 slice.52
  12.0 2.0 %collective-permute-done.1 = bf16[8,2,1,4096]{3,2,1,0:T(2,128)(2,1)S(1)} collective-permute-done((bf16[8,2,1,4096]{3,2,1,0:T(2,128)(2,1)S(1)}, bf16[8,2,1,4096]{3,2,1,0:T(2,128)(2,1)S(1)}, u32[]{:S(2)}, u32[]{:S(2)}) %collective-permute-start.1) | collective-permute-done | bytes 131104 | tf_op jit(solution)/shard_map/ppermute | solution.py:19
  14.0 0.4 broadcast_select_fusion
  14.4 5.3 %collective-permute-done = bf16[8,2,1,4096]{3,2,1,0:T(2,128)(2,1)S(1)} collective-permute-done((bf16[8,2,1,4096]{3,2,1,0:T(2,128)(2,1)S(1)}, bf16[8,2,1,4096]{3,2,1,0:T(2,128)(2,1)S(1)}, u32[]{:S(2)}, u32[]{:S(2)}) %collective-permute-start) | collective-permute-done | bytes 131104 | tf_op jit(solution)/shard_map/ppermute | solution.py:18
  19.7 2.3 %fusion.2 = bf16[8,2,4,4096]{3,2,1,0:T(4,128)(2,1)S(1)} fusion(bf16[8,2,4,4096]{3,2,1,0:T(4,128)(2,1)S(1)} %broadcast_select_fusion.1, bf16[8,2,4,1]{3,2,1,0:T(4,128)(2,1)S(1)} %collective-permute-done.3, bf16[8,2,4,1]{3,2,1,0:T(4,128)(2,1)S(1)} %collective-permute-done.2, bf16[8,2,1,4096]{3,2,1,0:T(2,128)(2,1)S(1)} %collective-permute-done, ...), kind=kLoop, calls=%fused_computation.5 | loop fusion | flops 6553600 | bytes 1704192 | tf_op jit(solution)/shard_map/convert_element_type | solution.py:66
  22.0 2.2 %fusion.7 = f32[8,2,4,32]{3,2,1,0:T(4,128)S(1)} fusion(bf16[8,2,4,4096]{3,2,1,0:T(4,128)(2,1)S(1)} %fusion.2, s32[32]{0:T(128)S(1)} %copy-done.3, s32[4096]{0:T(1024)S(1)} %iota_add_fusion), kind=kOutput, calls=%fused_computation.22 | convolution fusion | flops 18743296 | bytes 548992 | tf_op jit(solution)/shard_map/dot_general | solution.py:70
  24.3 2.3 %multiply_bitcast_fusion.1 = (f32[8,2,4,1,32]{4,2,1,0,3:T(4,128)S(1)}, f32[8,2,4,1,32]{4,2,1,0,3:T(4,128)S(1)}) fusion(f32[8,2,4,32]{3,2,1,0:T(4,128)S(1)} %fusion.7, f32[4,32]{1,0:T(4,128)S(1)} %get-tuple-element.16, f32[4,32]{1,0:T(4,128)S(1)} %get-tuple-element.15, bf16[8,2,4,4096]{3,2,1,0:T(4,128)(2,1)S(1)} %fusion.2, s32[32]{0:T(128)S(1)} %copy-done.3, ...), kind=kOutput, calls=%fused_computation.44 | convolution fusion | flops 18890752 | bytes 566400 | tf_op jit(solution)/shard_map/dot_general | solution.py:73
  26.6 0.2 copy.16
  26.8 0.9 %reshape.175 = f32[8,1,512]{2,1,0:T(1,128)} reshape(f32[32,2,2,4,8]{4,3,2,1,0:T(4,128)S(1)} %bitcast.33) | data formatting | bytes 32768
  27.7 5.8 %all-to-all-start = ((f32[8,1,512]{2,1,0:T(1,128)}), f32[8,1,512]{2,1,0:T(1,128)S(1)}, u32[]{:S(2)}, u32[]{:S(2)}) async-start(f32[8,1,512]{2,1,0:T(1,128)} %reshape.175), calls=%async_computation | async-start | bytes 32768 | tf_op jit(solution)/shard_map/all_to_all | solution.py:91
  33.6 6.4 %all-to-all-done = f32[8,1,512]{2,1,0:T(1,128)S(1)} async-done(((f32[8,1,512]{2,1,0:T(1,128)}), f32[8,1,512]{2,1,0:T(1,128)S(1)}, u32[]{:S(2)}, u32[]{:S(2)}) %all-to-all-start) | async-done | bytes 16416 | tf_op jit(solution)/shard_map/all_to_all | solution.py:91
  40.0 0.5 broadcast.207
  40.5 0.7 %reduce = f32[8,512]{1,0:T(8,128)S(1)} reduce(f32[8,1,512]{2,1,0:T(1,128)S(1)} %all-to-all-done, f32[]{:T(128)} %broadcast.207), dimensions={1}, to_apply=%all_to_all.13.reduce_sub_computation | reduce | bytes 32772 | tf_op jit(solution)/shard_map/all_to_all | solution.py:91
  41.2 0.3 reshape.176
  42.0 10.7 %psum.7 = bf16[8,2,32,2,4]{2,0,3,4,1:T(8,128)(2,1)S(1)} all-reduce(f32[8,2,32,2,4]{2,0,3,4,1:T(8,128)S(1)} %copy.19), channel_id=1, replica_groups=mesh['blk'=8,'lblk'=4] {'lblk'}, use_global_device_ids=true, to_apply=%region_0.1 | all-reduce | flops 4096 | bytes 24576 | tf_op jit(solution)/shard_map/psum | solution.py:92
  52.7 0.2 convolution_bitcast_fusion
  52.9 0.9 %copy.20 = f32[8,2,4,1024]{3,2,1,0:T(4,128)} copy(f32[8,2,4,1024]{3,0,1,2:T(8,128)S(1)} %fusion.12) | data formatting | bytes 524288 | tf_op jit(solution)/shard_map/jit(_where)/select_n | solution.py:42
  (24 shorter events, 1.0 us)
Async XLA Ops:
  0.0 0.7 %copy-start.1 = (s32[2,4]{1,0:T(2,128)S(1)}, s32[2,4]{1,0:T(2,128)}, u32[]{:S(2)}) copy-start(s32[2,4]{1,0:T(2,128)} %param.7) | copy-start | bytes 100
  0.0 0.7 %copy-start.2 = (s32[2,4]{1,0:T(2,128)S(1)}, s32[2,4]{1,0:T(2,128)}, u32[]{:S(2)}) copy-start(s32[2,4]{1,0:T(2,128)} %param.6) | copy-start | bytes 100
  2.8 11.2 %collective-permute-start.1 = (bf16[8,2,1,4096]{3,2,1,0:T(2,128)(2,1)S(1)}, bf16[8,2,1,4096]{3,2,1,0:T(2,128)(2,1)S(1)}, u32[]{:S(2)}, u32[]{:S(2)}) collective-permute-start(bf16[8,2,1,4096]{3,2,1,0:T(2,128)(2,1)S(1)} %get-tuple-element.5), channel_id=1, source_target_pairs={{4,0},{8,4},{12,8},{16,12},{20,16},{24,20},{28,24},{5,1},{9,5},{13... | collective-permute-start | bytes 393224 | tf_op jit(solution)/shard_map/ppermute | solution.py:19
  4.1 15.7 %collective-permute-start = (bf16[8,2,1,4096]{3,2,1,0:T(2,128)(2,1)S(1)}, bf16[8,2,1,4096]{3,2,1,0:T(2,128)(2,1)S(1)}, u32[]{:S(2)}, u32[]{:S(2)}) collective-permute-start(bf16[8,2,1,4096]{3,2,1,0:T(2,128)(2,1)S(1)} %get-tuple-element.6), channel_id=1, source_target_pairs={{0,4},{4,8},{8,12},{12,16},{16,20},{20,24},{24,28},{1,5},{5,9},{9,... | collective-permute-start | bytes 393224 | tf_op jit(solution)/shard_map/ppermute | solution.py:18
  9.7 4.7 %collective-permute-start.2 = (bf16[8,2,4,1]{3,2,1,0:T(4,128)(2,1)S(1)}, bf16[8,2,4,1]{3,2,1,0:T(4,128)(2,1)S(1)}, u32[]{:S(2)}, u32[]{:S(2)}) collective-permute-start(bf16[8,2,4,1]{3,2,1,0:T(4,128)(2,1)S(1)} %get-tuple-element.7), channel_id=1, source_target_pairs={{0,1},{1,2},{2,3},{3,0},{4,5},{5,6},{6,7},{7,4},{8,9},{9,10},{10,1... | collective-permute-start | bytes 392 | tf_op jit(solution)/shard_map/ppermute | solution.py:18
  9.8 1.7 %copy-start.3 = (s32[32]{0:T(128)S(1)}, s32[32]{0:T(128)}, u32[]{:S(2)}) copy-start(s32[32]{0:T(128)} %param.8) | copy-start | bytes 388
  9.8 4.6 %collective-permute-start.3 = (bf16[8,2,4,1]{3,2,1,0:T(4,128)(2,1)S(1)}, bf16[8,2,4,1]{3,2,1,0:T(4,128)(2,1)S(1)}, u32[]{:S(2)}, u32[]{:S(2)}) collective-permute-start(bf16[8,2,4,1]{3,2,1,0:T(4,128)(2,1)S(1)} %get-tuple-element.8), channel_id=1, source_target_pairs={{1,0},{2,1},{3,2},{0,3},{5,4},{6,5},{7,6},{4,7},{9,8},{10,9},{11,1... | collective-permute-start | bytes 392 | tf_op jit(solution)/shard_map/ppermute | solution.py:19
  26.6 7.0 %copy-start = (bf16[4,8,4,1024]{3,2,1,0:T(4,128)(2,1)S(1)}, bf16[4,8,4,1024]{3,2,1,0:T(4,128)(2,1)}, u32[]{:S(2)}) copy-start(bf16[4,8,4,1024]{3,2,1,0:T(4,128)(2,1)} %param.9) | copy-start | bytes 786436
  27.7 12.4 %all-to-all-start = ((f32[8,1,512]{2,1,0:T(1,128)}), f32[8,1,512]{2,1,0:T(1,128)S(1)}, u32[]{:S(2)}, u32[]{:S(2)}) async-start(f32[8,1,512]{2,1,0:T(1,128)} %reshape.175), calls=%async_computation | async-start | bytes 32768 | tf_op jit(solution)/shard_map/all_to_all | solution.py:91
where the time goes:
time: 54.1 us; the launch traced here: 53.8 us
  starting transfers between devices  14.4 us (27%)
  waiting for transfers between devices  13.7 us (25%)
  blocking collectives  10.7 us (20%)
  other arithmetic  5.17 us (10%)
  local copies, waits for them, and re-layouts  4.95 us (9%)
  matrix products  4.74 us (9%)
    psum x1, blocking collectives, local(): summed = lax.psum(spread, 'lblk')  10.7 us
    all_to_all x1, waiting for transfers between devices, local(): lax.all_to_all(partial_value, 'blk', split_axis=4, concat_axis=2, tiled=T...  6.4 us
    all_to_all x1, starting transfers between devices, local(): lax.all_to_all(partial_value, 'blk', split_axis=4, concat_axis=2, tiled=T...  5.78 us
    ppermute x2, starting transfers between devices, padded(): before = lax.ppermute(last, axis, up)  5.6 us
    ppermute x2, waiting for transfers between devices, padded(): before = lax.ppermute(last, axis, up)  5.33 us
    ppermute x2, starting transfers between devices, padded(): after = lax.ppermute(initial, axis, down)  3.01 us
    dot_general x1, matrix products, local(): jnp.dot(flat_rows, sin_table, preferred_element_type=jnp.float32)  2.29 us
    convert_element_type x1, other arithmetic, local(): smooth = (centre + DIFFUSION * total).astype(jnp.bfloat16)  2.27 us
  transfers between devices with their start and end apart: 5, of which 3 were waited for; matrix products, arithmetic and copies ran while one was open for 2% of the time, Pallas kernels for 0%

commit v1 on v0

--- a/solution.py
+++ b/solution.py
@@ -89,7 +89,11 @@
     degrees = column * degree_part + jnp.arange(degree_part, dtype=jnp.int32)
     legendre_rows = legendre.reshape(owned_count, -1, degree_part)
     spread = lax.all_to_all(partial_value, "blk", split_axis=4, concat_axis=2, tiled=True)
-    summed = lax.psum(spread, "lblk")
+    size = lax.axis_size("lblk")
+    summed, hop = (spread, 1)
+    while hop < size:
+        summed = summed + lax.ppermute(summed, "lblk", [(i_2, i_2 ^ hop) for i_2 in range(size)])
+        hop = 2 * hop
     fourier = summed.astype(jnp.bfloat16)
     result = legendre_section(fourier, legendre_rows, my_modes, degrees)
     return result

time: 54.1 us -> 49.1 us (0.908)
  blocking collectives: 10.7 us -> 0 us
  waiting for transfers between devices: 13.7 us -> 17 us
  starting transfers between devices: 14.4 us -> 16 us
  local copies, waits for them, and re-layouts: 4.95 us -> 5.58 us
    psum x1 -> x0, blocking collectives: 10.7 us -> none  [local(): summed = lax.psum(spread, 'lblk')]
    ppermute x0 -> x2, waiting for transfers between devices: none -> 3.75 us  [local(): lax.ppermute(summed, 'lblk', [(i_2, i_2 ^ hop) for i_2 in range(size)])]
    ppermute x0 -> x2, starting transfers between devices: none -> 1.6 us  [local(): lax.ppermute(summed, 'lblk', [(i_2, i_2 ^ hop) for i_2 in range(size)])]
    unnamed x10, local copies, waits for them, and re-layouts: 1.9 us -> 2.54 us
    ppermute x2, waiting for transfers between devices: 1.95 us -> 1.38 us  [padded(): after = lax.ppermute(initial, axis, down)]
  transfers between devices with their start and end apart: 5 -> 7, of which waited for: 3 -> 5; matrix products, arithmetic and copies ran while one was open for 2% -> 2% of each run, Pallas kernels for 0% -> 0%
where the time goes in v1:
time: 49.1 us; the launch traced here: 48.8 us
  waiting for transfers between devices  17 us (35%)
  starting transfers between devices  16 us (33%)
  local copies, waits for them, and re-layouts  5.58 us (11%)
  other arithmetic  5.19 us (11%)
  matrix products  4.74 us (10%)
    all_to_all x1, waiting for transfers between devices, local(): lax.all_to_all(partial_value, 'blk', split_axis=4, concat_axis=2, tiled=T...  6.58 us
    all_to_all x1, starting transfers between devices, local(): lax.all_to_all(partial_value, 'blk', split_axis=4, concat_axis=2, tiled=T...  5.78 us
    ppermute x2, starting transfers between devices, padded(): before = lax.ppermute(last, axis, up)  5.6 us
    ppermute x2, waiting for transfers between devices, padded(): before = lax.ppermute(last, axis, up)  5.33 us
    ppermute x2, waiting for transfers between devices, local(): lax.ppermute(summed, 'lblk', [(i_2, i_2 ^ hop) for i_2 in range(size)])  3.75 us
    ppermute x2, starting transfers between devices, padded(): after = lax.ppermute(initial, axis, down)  3.02 us
    unnamed x10, local copies, waits for them, and re-layouts  2.54 us
    dot_general x1, matrix products, local(): jnp.dot(flat_rows, sin_table, preferred_element_type=jnp.float32)  2.29 us
  transfers between devices with their start and end apart: 7, of which 5 were waited for; matrix products, arithmetic and copies ran while one was open for 2% of the time, Pallas kernels for 0%

profile of v1, /device:TPU:0, one launch (start us, length us, event | category | flops | bytes accessed | tf_op | source)
XLA Modules:
  0.0 48.8 jit_solution(423914419627697912)
XLA Ops:
  0.0 0.7 %copy-done.1 = s32[2,4]{1,0:T(2,128)S(1)} copy-done((s32[2,4]{1,0:T(2,128)S(1)}, s32[2,4]{1,0:T(2,128)}, u32[]{:S(2)}) %copy-start.1) | copy-done | bytes 56
  0.9 1.3 %broadcast_select_fusion.1 = bf16[8,2,4,4096]{3,2,1,0:T(4,128)(2,1)S(1)} fusion(bf16[8,2,4,4096]{3,2,1,0:T(4,128)(2,1)} %param.5, pred[2,4,4096]{2,1,0:T(4,128)(4,1)S(1)} %fusion.16), kind=kLoop, calls=%fused_computation.20 | loop fusion | flops 262144 | bytes 1081344 | tf_op jit(solution)/shard_map/jit(_where)/select_n | solution.py:53
  2.2 0.6 %fusion.38 = (bf16[8,2,1,4096]{3,2,1,0:T(2,128)(2,1)S(1)}, bf16[8,2,1,4096]{3,2,1,0:T(2,128)(2,1)S(1)}) fusion(bf16[8,2,4,4096]{3,2,1,0:T(4,128)(2,1)S(1)} %broadcast_select_fusion.1), kind=kLoop, calls=%fused_computation.71 | loop fusion | bytes 524288 | tf_op jit(solution)/shard_map/slice | solution.py:17
  2.8 1.3 %collective-permute-start.1 = (bf16[8,2,1,4096]{3,2,1,0:T(2,128)(2,1)S(1)}, bf16[8,2,1,4096]{3,2,1,0:T(2,128)(2,1)S(1)}, u32[]{:S(2)}, u32[]{:S(2)}) collective-permute-start(bf16[8,2,1,4096]{3,2,1,0:T(2,128)(2,1)S(1)} %get-tuple-element.5), channel_id=1, source_target_pairs={{4,0},{8,4},{12,8},{16,12},{20,16},{24,20},{28,24},{5,1},{9,5},{13... | collective-permute-start | bytes 393224 | tf_op jit(solution)/shard_map/ppermute | solution.py:19
  4.1 5.5 %collective-permute-start = (bf16[8,2,1,4096]{3,2,1,0:T(2,128)(2,1)S(1)}, bf16[8,2,1,4096]{3,2,1,0:T(2,128)(2,1)S(1)}, u32[]{:S(2)}, u32[]{:S(2)}) collective-permute-start(bf16[8,2,1,4096]{3,2,1,0:T(2,128)(2,1)S(1)} %get-tuple-element.6), channel_id=1, source_target_pairs={{0,4},{4,8},{8,12},{12,16},{16,20},{20,24},{24,28},{1,5},{5,9},{9,... | collective-permute-start | bytes 393224 | tf_op jit(solution)/shard_map/ppermute | solution.py:18
  9.8 1.7 %collective-permute-start.3 = (bf16[8,2,4,1]{3,2,1,0:T(4,128)(2,1)S(1)}, bf16[8,2,4,1]{3,2,1,0:T(4,128)(2,1)S(1)}, u32[]{:S(2)}, u32[]{:S(2)}) collective-permute-start(bf16[8,2,4,1]{3,2,1,0:T(4,128)(2,1)S(1)} %get-tuple-element.8), channel_id=1, source_target_pairs={{1,0},{2,1},{3,2},{0,3},{5,4},{6,5},{7,6},{4,7},{9,8},{10,9},{11,1... | collective-permute-start | bytes 392 | tf_op jit(solution)/shard_map/ppermute | solution.py:19
  11.5 0.3 slice.52
  11.8 0.6 %copy-done.3 = s32[32]{0:T(128)S(1)} copy-done((s32[32]{0:T(128)S(1)}, s32[32]{0:T(128)}, u32[]{:S(2)}) %copy-start.3) | copy-done | bytes 152
  12.6 1.4 %collective-permute-done.1 = bf16[8,2,1,4096]{3,2,1,0:T(2,128)(2,1)S(1)} collective-permute-done((bf16[8,2,1,4096]{3,2,1,0:T(2,128)(2,1)S(1)}, bf16[8,2,1,4096]{3,2,1,0:T(2,128)(2,1)S(1)}, u32[]{:S(2)}, u32[]{:S(2)}) %collective-permute-start.1) | collective-permute-done | bytes 131104 | tf_op jit(solution)/shard_map/ppermute | solution.py:19
  14.0 0.4 broadcast_select_fusion
  14.4 5.3 %collective-permute-done = bf16[8,2,1,4096]{3,2,1,0:T(2,128)(2,1)S(1)} collective-permute-done((bf16[8,2,1,4096]{3,2,1,0:T(2,128)(2,1)S(1)}, bf16[8,2,1,4096]{3,2,1,0:T(2,128)(2,1)S(1)}, u32[]{:S(2)}, u32[]{:S(2)}) %collective-permute-start) | collective-permute-done | bytes 131104 | tf_op jit(solution)/shard_map/ppermute | solution.py:18
  19.7 2.3 %fusion.2 = bf16[8,2,4,4096]{3,2,1,0:T(4,128)(2,1)S(1)} fusion(bf16[8,2,4,4096]{3,2,1,0:T(4,128)(2,1)S(1)} %broadcast_select_fusion.1, bf16[8,2,4,1]{3,2,1,0:T(4,128)(2,1)S(1)} %collective-permute-done.3, bf16[8,2,4,1]{3,2,1,0:T(4,128)(2,1)S(1)} %collective-permute-done.2, bf16[8,2,1,4096]{3,2,1,0:T(2,128)(2,1)S(1)} %collective-permute-done, ...), kind=kLoop, calls=%fused_computation.5 | loop fusion | flops 6553600 | bytes 1704192 | tf_op jit(solution)/shard_map/convert_element_type | solution.py:66
  22.0 2.2 %fusion.7 = f32[8,2,4,32]{3,2,1,0:T(4,128)S(1)} fusion(bf16[8,2,4,4096]{3,2,1,0:T(4,128)(2,1)S(1)} %fusion.2, s32[32]{0:T(128)S(1)} %copy-done.3, s32[4096]{0:T(1024)S(1)} %iota_add_fusion), kind=kOutput, calls=%fused_computation.22 | convolution fusion | flops 18743296 | bytes 548992 | tf_op jit(solution)/shard_map/dot_general | solution.py:70
  24.3 2.3 %multiply_bitcast_fusion.1 = (f32[8,2,4,1,32]{4,2,1,0,3:T(4,128)S(1)}, f32[8,2,4,1,32]{4,2,1,0,3:T(4,128)S(1)}) fusion(f32[8,2,4,32]{3,2,1,0:T(4,128)S(1)} %fusion.7, f32[4,32]{1,0:T(4,128)S(1)} %get-tuple-element.16, f32[4,32]{1,0:T(4,128)S(1)} %get-tuple-element.15, bf16[8,2,4,4096]{3,2,1,0:T(4,128)(2,1)S(1)} %fusion.2, s32[32]{0:T(128)S(1)} %copy-done.3, ...), kind=kOutput, calls=%fused_computation.45 | convolution fusion | flops 18890752 | bytes 566400 | tf_op jit(solution)/shard_map/dot_general | solution.py:73
  26.8 0.9 %reshape.175 = f32[8,1,512]{2,1,0:T(1,128)} reshape(f32[32,2,2,4,8]{4,3,2,1,0:T(4,128)S(1)} %bitcast.33) | data formatting | bytes 32768
  27.7 5.8 %all-to-all-start = ((f32[8,1,512]{2,1,0:T(1,128)}), f32[8,1,512]{2,1,0:T(1,128)S(1)}, u32[]{:S(2)}, u32[]{:S(2)}) async-start(f32[8,1,512]{2,1,0:T(1,128)} %reshape.175), calls=%async_computation | async-start | bytes 32768 | tf_op jit(solution)/shard_map/all_to_all | solution.py:91
  33.4 6.6 %all-to-all-done = f32[8,1,512]{2,1,0:T(1,128)S(1)} async-done(((f32[8,1,512]{2,1,0:T(1,128)}), f32[8,1,512]{2,1,0:T(1,128)S(1)}, u32[]{:S(2)}, u32[]{:S(2)}) %all-to-all-start) | async-done | bytes 16416 | tf_op jit(solution)/shard_map/all_to_all | solution.py:91
  40.0 0.5 %broadcast.207 = f32[]{:T(128)} broadcast(f32[]{:T(128)} %constant.147), dimensions={} | broadcast | bytes 8 | tf_op jit(solution)/shard_map/all_to_all | solution.py:91
  40.5 0.7 %reduce = f32[8,512]{1,0:T(8,128)S(1)} reduce(f32[8,1,512]{2,1,0:T(1,128)S(1)} %all-to-all-done, f32[]{:T(128)} %broadcast.207), dimensions={1}, to_apply=%all_to_all.13.reduce_sub_computation | reduce | bytes 32772 | tf_op jit(solution)/shard_map/all_to_all | solution.py:91
  41.2 0.3 reshape.176
  42.1 1.1 %collective-permute-done.4 = f32[8,2,32,2,4]{2,0,3,4,1:T(8,128)S(1)} collective-permute-done((f32[8,2,32,2,4]{2,0,3,4,1:T(8,128)S(1)}, f32[8,2,32,2,4]{2,0,3,4,1:T(8,128)S(1)}, u32[]{:S(2)}, u32[]{:S(2)}) %collective-permute-start.4) | collective-permute-done | bytes 16416 | tf_op jit(solution)/shard_map/ppermute | solution.py:95
  43.3 1.6 %collective-permute-start.5 = (f32[8,2,32,2,4]{2,0,3,4,1:T(8,128)S(1)}, f32[8,2,32,2,4]{2,0,3,4,1:T(8,128)S(1)}, u32[]{:S(2)}, u32[]{:S(2)}) collective-permute-start(f32[8,2,32,2,4]{2,0,3,4,1:T(8,128)S(1)} %add.118), channel_id=1, source_target_pairs={{0,2},{1,3},{2,0},{3,1},{4,6},{5,7},{6,4},{7,5},{8,10},{9,11},{10,... | collective-permute-start | bytes 49160 | tf_op jit(solution)/shard_map/ppermute | solution.py:95
  45.0 2.6 %collective-permute-done.5 = f32[8,2,32,2,4]{2,0,3,4,1:T(8,128)S(1)} collective-permute-done((f32[8,2,32,2,4]{2,0,3,4,1:T(8,128)S(1)}, f32[8,2,32,2,4]{2,0,3,4,1:T(8,128)S(1)}, u32[]{:S(2)}, u32[]{:S(2)}) %collective-permute-start.5) | collective-permute-done | bytes 16416 | tf_op jit(solution)/shard_map/ppermute | solution.py:95
  47.9 0.9 %copy.22 = f32[8,2,4,1024]{3,2,1,0:T(4,128)} copy(f32[8,2,4,1024]{3,0,1,2:T(8,128)S(1)} %fusion.12) | data formatting | bytes 524288 | tf_op jit(solution)/shard_map/jit(_where)/select_n | solution.py:42
  (29 shorter events, 1.7 us)
Async XLA Ops:
  0.0 0.7 %copy-start.1 = (s32[2,4]{1,0:T(2,128)S(1)}, s32[2,4]{1,0:T(2,128)}, u32[]{:S(2)}) copy-start(s32[2,4]{1,0:T(2,128)} %param.7) | copy-start | bytes 100
  0.0 0.7 %copy-start.2 = (s32[2,4]{1,0:T(2,128)S(1)}, s32[2,4]{1,0:T(2,128)}, u32[]{:S(2)}) copy-start(s32[2,4]{1,0:T(2,128)} %param.6) | copy-start | bytes 100
  2.8 11.2 %collective-permute-start.1 = (bf16[8,2,1,4096]{3,2,1,0:T(2,128)(2,1)S(1)}, bf16[8,2,1,4096]{3,2,1,0:T(2,128)(2,1)S(1)}, u32[]{:S(2)}, u32[]{:S(2)}) collective-permute-start(bf16[8,2,1,4096]{3,2,1,0:T(2,128)(2,1)S(1)} %get-tuple-element.5), channel_id=1, source_target_pairs={{4,0},{8,4},{12,8},{16,12},{20,16},{24,20},{28,24},{5,1},{9,5},{13... | collective-permute-start | bytes 393224 | tf_op jit(solution)/shard_map/ppermute | solution.py:19
  4.1 15.7 %collective-permute-start = (bf16[8,2,1,4096]{3,2,1,0:T(2,128)(2,1)S(1)}, bf16[8,2,1,4096]{3,2,1,0:T(2,128)(2,1)S(1)}, u32[]{:S(2)}, u32[]{:S(2)}) collective-permute-start(bf16[8,2,1,4096]{3,2,1,0:T(2,128)(2,1)S(1)} %get-tuple-element.6), channel_id=1, source_target_pairs={{0,4},{4,8},{8,12},{12,16},{16,20},{20,24},{24,28},{1,5},{5,9},{9,... | collective-permute-start | bytes 393224 | tf_op jit(solution)/shard_map/ppermute | solution.py:18
  9.7 4.7 %collective-permute-start.2 = (bf16[8,2,4,1]{3,2,1,0:T(4,128)(2,1)S(1)}, bf16[8,2,4,1]{3,2,1,0:T(4,128)(2,1)S(1)}, u32[]{:S(2)}, u32[]{:S(2)}) collective-permute-start(bf16[8,2,4,1]{3,2,1,0:T(4,128)(2,1)S(1)} %get-tuple-element.7), channel_id=1, source_target_pairs={{0,1},{1,2},{2,3},{3,0},{4,5},{5,6},{6,7},{7,4},{8,9},{9,10},{10,1... | collective-permute-start | bytes 392 | tf_op jit(solution)/shard_map/ppermute | solution.py:18
  9.8 4.6 %collective-permute-start.3 = (bf16[8,2,4,1]{3,2,1,0:T(4,128)(2,1)S(1)}, bf16[8,2,4,1]{3,2,1,0:T(4,128)(2,1)S(1)}, u32[]{:S(2)}, u32[]{:S(2)}) collective-permute-start(bf16[8,2,4,1]{3,2,1,0:T(4,128)(2,1)S(1)} %get-tuple-element.8), channel_id=1, source_target_pairs={{1,0},{2,1},{3,2},{0,3},{5,4},{6,5},{7,6},{4,7},{9,8},{10,9},{11,1... | collective-permute-start | bytes 392 | tf_op jit(solution)/shard_map/ppermute | solution.py:19
  11.8 0.7 %copy-start.3 = (s32[32]{0:T(128)S(1)}, s32[32]{0:T(128)}, u32[]{:S(2)}) copy-start(s32[32]{0:T(128)} %param.8) | copy-start | bytes 388
  27.7 12.4 %all-to-all-start = ((f32[8,1,512]{2,1,0:T(1,128)}), f32[8,1,512]{2,1,0:T(1,128)S(1)}, u32[]{:S(2)}, u32[]{:S(2)}) async-start(f32[8,1,512]{2,1,0:T(1,128)} %reshape.175), calls=%async_computation | async-start | bytes 32768 | tf_op jit(solution)/shard_map/all_to_all | solution.py:91
  41.8 3.1 %copy-start = (bf16[4,8,4,1024]{3,2,1,0:T(4,128)(2,1)S(1)}, bf16[4,8,4,1024]{3,2,1,0:T(4,128)(2,1)}, u32[]{:S(2)}) copy-start(bf16[4,8,4,1024]{3,2,1,0:T(4,128)(2,1)} %param.9) | copy-start | bytes 786436
  42.0 1.3 %collective-permute-start.4 = (f32[8,2,32,2,4]{2,0,3,4,1:T(8,128)S(1)}, f32[8,2,32,2,4]{2,0,3,4,1:T(8,128)S(1)}, u32[]{:S(2)}, u32[]{:S(2)}) collective-permute-start(f32[8,2,32,2,4]{2,0,3,4,1:T(8,128)S(1)} %copy.21), channel_id=1, source_target_pairs={{0,1},{1,0},{2,3},{3,2},{4,5},{5,4},{6,7},{7,6},{8,9},{9,8},{10,11... | collective-permute-start | bytes 49160 | tf_op jit(solution)/shard_map/ppermute | solution.py:95
  43.3 4.3 %collective-permute-start.5 = (f32[8,2,32,2,4]{2,0,3,4,1:T(8,128)S(1)}, f32[8,2,32,2,4]{2,0,3,4,1:T(8,128)S(1)}, u32[]{:S(2)}, u32[]{:S(2)}) collective-permute-start(f32[8,2,32,2,4]{2,0,3,4,1:T(8,128)S(1)} %add.118), channel_id=1, source_target_pairs={{0,2},{1,3},{2,0},{3,1},{4,6},{5,7},{6,4},{7,5},{8,10},{9,11},{10,... | collective-permute-start | bytes 49160 | tf_op jit(solution)/shard_map/ppermute | solution.py:95
